TPU v7x, 32 devices: a whole 2x2x4 slice. The times are simulated.
32 devices in a mesh: seq: 8 (over y, x, core), expert: 4 (over z).
Axes of the slice: x: 2, y: 2, z: 4, core: 2. Of those that a mesh axis runs over, the one named last changes fastest.
Arguments:
- x_in: bfloat16 [1024, 4096], P('seq', 'expert'), may hold values from -6 to 6
- z_in: bfloat16 [1024, 4096], P('seq', 'expert'), may hold values from -6 to 6
- dt_raw: float32 [1024, 4096], P('seq', 'expert'), may hold values from -4 to 4
- bc_in: float32 [2, 16, 1024], P(None, None, 'seq'), may hold values from -6 to 6
- a_log: float32 [16, 4096], P(None, 'expert'), may hold values from -2 to 1.5
- conv_weight: float32 [4, 4096], P(None, 'expert'), may hold values from -3 to 3
- conv_bias: float32 [4096], P('expert'), may hold values from -3 to 3
- skip_gain: float32 [4096], P('expert'), may hold values from 0.25 to 1.75
- dt_bias: float32 [4096], P('expert'), may hold values from -6 to -1
- out_weight: bfloat16 [4096, 2048], P('expert'), may hold values from -0.09375 to 0.09375
- resid: bfloat16 [1024, 2048], P(('seq', 'expert')), may hold values from -6 to 6
- w_gate: bfloat16 [4, 2048, 7168], P('expert', None, 'seq'), may hold values from -0.125 to 0.125
- w_up: bfloat16 [4, 2048, 7168], P('expert', None, 'seq'), may hold values from -0.125 to 0.125
- w_down: bfloat16 [4, 7168, 2048], P('expert', 'seq'), may hold values from -0.0625 to 0.0625
- route_ids: int32 [1024, 2], P(('seq', 'expert')), may hold values from 0 to 3, all different within a row; in each aligned block of 32 rows (0 to 31, 32 to 63, ...) at most 32 rows name the same one
- route_weight: float32 [1024, 2], P(('seq', 'expert')), may hold values from 0.2 to 0.8
- grad_mix: bfloat16 [1024, 2048], P('seq'), may hold values from -6 to 6
Outputs:
- layer_out: bfloat16 [1024, 2048], P(('seq', 'expert'))
- grad_x: float32 [1024, 4096], P('seq', 'expert')
- grad_z: float32 [1024, 4096], P('seq', 'expert')
- grad_dt: float32 [1024, 4096], P('seq', 'expert')
- grad_bc: float32 [2, 16, 1024], P(None, None, 'seq')
- grad_alog: float32 [16, 4096], P(None, 'expert')
- grad_conv: float32 [4, 4096], P(None, 'expert')
- grad_chan: float32 [3, 4096], P(None, 'expert')
Inputs may be any that keep to these rules, and one draw needn't show every extreme that they name: `route_ids`: within the 32 rows of one device no expert is named by more than 32 rows; some expert is named by exactly 32. The two experts of a token differ.
All inputs are finite; a program needn't handle non-finite values.
Results may differ from a plain program's by a relative error of at most 0.028.
Values may be sent and summed in bfloat16 or wider, within the bound.
A program may use at most 128 MiB of HBM per device.

v0:
```python
import jax
import jax.numpy as jnp
from jax import lax
from jax.experimental import pallas as pl
from jax.experimental.pallas import tpu as pltpu
from jax.sharding import PartitionSpec as P

KW = 4
SUB = 8
LANES = 128


def shifted(x, axis, by):
    peers = lax.axis_size(axis)
    pairs = [(i, i + by) for i in range(peers) if 0 <= i + by < peers]
    return lax.ppermute(x, axis, pairs)


def wide(tile, width):
    return jnp.concatenate([tile] * (width // tile.shape[1]), axis=1)


def folded(value):
    total = value[:, :LANES]
    for at in range(LANES, value.shape[1], LANES):
        total = total + value[:, at : at + LANES]
    return total


def totals_kernel(step_ref, drive_ref, grad_ref, b_ref, c_ref, rate_ref, out_ref):
    rate = rate_ref[...]
    width = rate.shape[1]

    def advance(i, carry):
        state, passed, leaving = carry
        for j in range(SUB):
            decay = jnp.exp(step_ref[i, j : j + 1, :] * rate)
            state = decay * state + drive_ref[i, j : j + 1, :] * wide(b_ref[i, j], width)
            passed = passed * decay
            leaving = leaving + passed * (grad_ref[i, j : j + 1, :] * wide(c_ref[i, j], width))
        return (state, passed, leaving)

    zero = jnp.zeros_like(rate)
    state, passed, leaving = lax.fori_loop(
        0, step_ref.shape[0], advance, (zero, jnp.ones_like(rate), zero)
    )
    out_ref[0] = passed.astype(out_ref.dtype)
    out_ref[1] = state.astype(out_ref.dtype)
    out_ref[2] = leaving.astype(out_ref.dtype)


def forward_kernel(step_ref, drive_ref, b_ref, c_ref, rate_ref, start_ref, y_ref):
    rate = rate_ref[...]
    width = rate.shape[1]

    def advance(i, state):
        for j in range(SUB):
            decay = jnp.exp(step_ref[i, j : j + 1, :] * rate)
            state = decay * state + drive_ref[i, j : j + 1, :] * wide(b_ref[i, j], width)
            y_ref[i, j : j + 1, :] = jnp.sum(
                wide(c_ref[i, j], width) * state, axis=0, keepdims=True
            )
        return state

    lax.fori_loop(0, step_ref.shape[0], advance, start_ref[...])


def backward_kernel(
    step_ref,
    drive_ref,
    conv_ref,
    grad_ref,
    b_ref,
    c_ref,
    rate_ref,
    start_ref,
    arriving_ref,
    step_out_ref,
    conv_out_ref,
    b_out_ref,
    c_out_ref,
    alog_ref,
    states,
):
    rate = rate_ref[...]
    width = rate.shape[1]
    groups = step_ref.shape[0]

    @pl.when(pl.program_id(0) == 0)
    def _():
        b_out_ref[...] = jnp.zeros_like(b_out_ref)
        c_out_ref[...] = jnp.zeros_like(c_out_ref)

    states[0] = start_ref[...]

    def advance(i, state):
        for j in range(SUB):
            decay = jnp.exp(step_ref[i, j : j + 1, :] * rate)
            state = decay * state + drive_ref[i, j : j + 1, :] * wide(b_ref[i, j], width)
            states[i * SUB + j + 1] = state
        return state

    lax.fori_loop(0, groups, advance, start_ref[...])

    def retreat(k, carry):
        flow, alog_sum = carry
        i = groups - 1 - k
        for j in reversed(range(SUB)):
            at = i * SUB + j
            step_now = step_ref[i, j : j + 1, :]
            grad_now = grad_ref[i, j : j + 1, :]
            decay = jnp.exp(step_now * rate)
            adjoint = wide(c_ref[i, j], width) * grad_now + flow
            flow = decay * adjoint
            held = flow * states[at]
            alog_sum = alog_sum + step_now * held
            into_drive = jnp.sum(adjoint * wide(b_ref[i, j], width), axis=0, keepdims=True)
            step_out_ref[i, j : j + 1, :] = (
                jnp.sum(rate * held, axis=0, keepdims=True)
                + conv_ref[i, j : j + 1, :] * into_drive
            )
            conv_out_ref[i, j : j + 1, :] = step_now * into_drive
            b_out_ref[i, j] += folded(adjoint * drive_ref[i, j : j + 1, :])
            c_out_ref[i, j] += folded(grad_now * states[at + 1])
        return (flow, alog_sum)

    _, alog_sum = lax.fori_loop(0, groups, retreat, (arriving_ref[...], jnp.zeros_like(rate)))
    alog_ref[...] = alog_sum * rate


def sweeps(length, channels, states):
    block = min(512, channels)
    groups = length // SUB
    rows = pl.BlockSpec((groups, SUB, block), lambda k: (0, 0, k))
    spread = pl.BlockSpec((groups, SUB, states, LANES), lambda k: (0, 0, 0, 0))
    column = pl.BlockSpec((states, block), lambda k: (0, k))
    grid = (channels // block,)
    f32 = jnp.float32
    row_shape = jax.ShapeDtypeStruct((groups, SUB, channels), f32)
    spread_shape = jax.ShapeDtypeStruct((groups, SUB, states, LANES), f32)
    column_shape = jax.ShapeDtypeStruct((states, channels), f32)
    totals = pl.pallas_call(
        totals_kernel,
        grid=grid,
        in_specs=[rows, rows, rows, spread, spread, column],
        out_specs=pl.BlockSpec((3, states, block), lambda k: (0, 0, k)),
        out_shape=jax.ShapeDtypeStruct((3, states, channels), jnp.bfloat16),
        name="totals",
    )
    forward = pl.pallas_call(
        forward_kernel,
        grid=grid,
        in_specs=[rows, rows, spread, spread, column, column],
        out_specs=rows,
        out_shape=row_shape,
        name="forward",
    )
    backward = pl.pallas_call(
        backward_kernel,
        grid=grid,
        in_specs=[rows, rows, rows, rows, spread, spread, column, column, column],
        out_specs=[rows, rows, spread, spread, column],
        out_shape=[row_shape, row_shape, spread_shape, spread_shape, column_shape],
        scratch_shapes=[pltpu.VMEM((length + 1, states, block), f32)],
        name="backward",
    )
    return totals, forward, backward


def entering(everything):
    peers, here = everything.shape[0], lax.axis_index("seq")
    values = everything.astype(jnp.float32)
    start = jnp.zeros_like(values[0, 0])
    arriving = jnp.zeros_like(start)
    for k in range(peers):
        start = jnp.where(k < here, values[k, 0] * start + values[k, 1], start)
        back = peers - 1 - k
        arriving = jnp.where(back > here, values[back, 0] * arriving + values[back, 2], arriving)
    return start, arriving


def dense_experts(partial_value, resid, w_gate, w_up, w_down, route_ids, route_weight):
    rows = resid.shape[0]
    experts = lax.axis_size("expert")
    mine = lax.axis_index("expert")
    chosen = route_ids[:, :, None] == jnp.arange(experts, dtype=jnp.int32)[None, None, :]
    share = jnp.sum(jnp.where(chosen, route_weight[:, :, None], 0.0), axis=1)
    every_share = lax.all_gather(share, ("seq", "expert"), axis=0, tiled=True)
    is_mine = jnp.arange(experts, dtype=jnp.int32)[None, :] == mine
    scale = jnp.sum(jnp.where(is_mine, every_share, 0.0), axis=1, keepdims=True)
    group_resid = lax.all_gather(resid, "expert", axis=0, tiled=True)
    mixed = lax.psum(partial_value, "expert")
    hidden_in = (group_resid.astype(jnp.float32) + mixed.astype(jnp.float32)).astype(jnp.bfloat16)
    piece = lax.all_gather(hidden_in, "seq", axis=0, tiled=True)
    gate = jnp.dot(piece, w_gate[0], preferred_element_type=jnp.float32)
    upper = jnp.dot(piece, w_up[0], preferred_element_type=jnp.float32)
    hidden = (jax.nn.silu(gate) * upper).astype(jnp.bfloat16)
    part = jnp.dot(hidden, w_down[0], preferred_element_type=jnp.float32)
    part = (part * scale).astype(jnp.bfloat16)
    group_sum = lax.psum_scatter(part, "seq", scatter_dimension=0, tiled=True)
    moe = lax.psum_scatter(group_sum, "expert", scatter_dimension=0, tiled=True)
    own = lax.dynamic_slice_in_dim(hidden_in, mine * rows, rows, 0)
    return (own.astype(jnp.float32) + moe.astype(jnp.float32)).astype(jnp.bfloat16)


def routed_experts(partial_value, resid, w_gate, w_up, w_down, route_ids, route_weight):
    rows = resid.shape[0]
    mixed = lax.psum(partial_value, "expert").astype(jnp.float32)
    own = lax.dynamic_slice_in_dim(mixed, lax.axis_index("expert") * rows, rows, 0)
    hidden_in = (resid.astype(jnp.float32) + own).astype(jnp.bfloat16)
    experts = lax.axis_size("expert")
    capacity = 4 * rows // experts
    flat_ids = route_ids.reshape(-1)
    onehot = (flat_ids[:, None] == jnp.arange(experts, dtype=jnp.int32)[None, :]).astype(jnp.int32)
    rank = jnp.sum(jnp.cumsum(onehot, axis=0) * onehot, axis=1) - 1
    slot = flat_ids * capacity + rank
    placing = (jnp.arange(experts * capacity, dtype=jnp.int32)[:, None] == slot[None, :]).astype(
        jnp.bfloat16
    )
    doubled = jnp.repeat(hidden_in, 2, axis=0)
    outgoing = jnp.dot(placing, doubled, preferred_element_type=jnp.float32).astype(jnp.bfloat16)
    incoming = lax.all_to_all(outgoing, "expert", split_axis=0, concat_axis=0, tiled=True)
    piece = lax.all_gather(incoming, "seq", axis=0, tiled=True)
    gate = jnp.dot(piece, w_gate[0], preferred_element_type=jnp.float32)
    upper = jnp.dot(piece, w_up[0], preferred_element_type=jnp.float32)
    hidden = (jax.nn.silu(gate) * upper).astype(jnp.bfloat16)
    expert_sum = lax.psum_scatter(
        jnp.dot(hidden, w_down[0], preferred_element_type=jnp.float32).astype(jnp.bfloat16),
        "seq",
        scatter_dimension=0,
        tiled=True,
    )
    returned = lax.all_to_all(expert_sum, "expert", split_axis=0, concat_axis=0, tiled=True)
    picked = lax.dot_general(
        placing, returned, (((0,), (0,)), ((), ())), preferred_element_type=jnp.float32
    )
    picked = picked.reshape(rows, 2, -1)
    moe = picked[:, 0] * route_weight[:, 0:1] + picked[:, 1] * route_weight[:, 1:2]
    return (hidden_in.astype(jnp.float32) + moe).astype(jnp.bfloat16)


def local(
    x_in,
    z_in,
    dt_raw,
    bc_in,
    a_log,
    conv_weight,
    conv_bias,
    skip_gain,
    dt_bias,
    out_weight,
    resid,
    w_gate,
    w_up,
    w_down,
    route_ids,
    route_weight,
    grad_mix,
):
    length, channels = x_in.shape
    states = a_log.shape[0]
    rim = KW - 1
    x_val = x_in.astype(jnp.float32)
    z_val = z_in.astype(jnp.float32)
    before = shifted(x_in[length - rim :], "seq", 1)
    padded = jnp.concatenate([before.astype(jnp.float32), x_val], axis=0)
    pre = conv_bias[None, :] + conv_weight[0][None, :] * padded[0:length]
    for tap in range(1, KW):
        pre = pre + conv_weight[tap][None, :] * padded[tap : tap + length]
    conv_sig = jax.nn.sigmoid(pre)
    conv_out = pre * conv_sig
    step = jax.nn.softplus(dt_raw + dt_bias[None, :])
    rate = -jnp.exp(a_log)
    drive = step * conv_out
    z_sig = jax.nn.sigmoid(z_val)
    back_mix = lax.dot_general(
        grad_mix, out_weight, (((1,), (1,)), ((), ())), preferred_element_type=jnp.float32
    )
    grad_y = back_mix * z_val * z_sig

    def grouped(array):
        return array.reshape(length // SUB, SUB, channels)

    def flat(array):
        return array.reshape(length, channels)

    spread = jnp.broadcast_to(
        bc_in.transpose(0, 2, 1)[:, :, :, None], (2, length, states, LANES)
    ).reshape(2, length // SUB, SUB, states, LANES)
    b_wide, c_wide = spread[0], spread[1]
    totals, forward, backward = sweeps(length, channels, states)
    step_g, drive_g, grad_g, conv_g = (grouped(a) for a in (step, drive, grad_y, conv_out))
    own_totals = totals(step_g, drive_g, grad_g, b_wide, c_wide, rate)
    start, arriving = entering(lax.all_gather(own_totals, "seq"))
    y_val = flat(forward(step_g, drive_g, b_wide, c_wide, rate, start))
    y_val = y_val + skip_gain[None, :] * conv_out
    gated = (y_val * z_val * z_sig).astype(jnp.bfloat16)
    partial_value = jnp.dot(gated, out_weight, preferred_element_type=jnp.float32).astype(
        jnp.bfloat16
    )
    experts = dense_experts if lax.axis_size("expert") <= 4 else routed_experts
    layer_out = experts(partial_value, resid, w_gate, w_up, w_down, route_ids, route_weight)
    grad_z = back_mix * y_val * z_sig * (1.0 + z_val * (1.0 - z_sig))
    grad_step, conv_part_grad, grad_b, grad_c, grad_alog_local = backward(
        step_g, drive_g, conv_g, grad_g, b_wide, c_wide, rate, start, arriving
    )
    grad_step, conv_part_grad = flat(grad_step), flat(conv_part_grad)
    grad_conv_out = skip_gain[None, :] * grad_y + conv_part_grad
    grad_skip = jnp.sum(grad_y * conv_out, axis=0)
    grad_dt = grad_step * jax.nn.sigmoid(dt_raw + dt_bias[None, :])
    grad_pre = grad_conv_out * (conv_sig * (1.0 + pre * (1.0 - conv_sig)))
    after = shifted(grad_pre[:rim], "seq", -1)
    grad_pad = jnp.concatenate([grad_pre, after], axis=0)
    grad_x = conv_weight[rim][None, :] * grad_pad[0:length]
    for tap in range(rim):
        grad_x = grad_x + conv_weight[tap][None, :] * grad_pad[rim - tap : rim - tap + length]
    grad_taps = jnp.stack(
        [jnp.sum(grad_pre * padded[tap : tap + length], axis=0) for tap in range(KW)]
    )
    channel_grads = jnp.stack([jnp.sum(grad_pre, axis=0), grad_skip, jnp.sum(grad_dt, axis=0)])
    sums = lax.psum(jnp.concatenate([grad_alog_local, grad_taps, channel_grads], axis=0), "seq")
    grad_alog = sums[:states]
    grad_conv = sums[states : states + KW]
    grad_chan = sums[states + KW :]
    grad_bc = jnp.stack([jnp.sum(grad_b, axis=-1), jnp.sum(grad_c, axis=-1)])
    grad_bc = lax.psum(grad_bc.reshape(2, length, states).transpose(0, 2, 1), "expert")
    return (layer_out, grad_x, grad_z, grad_dt, grad_bc, grad_alog, grad_conv, grad_chan)


def solution(mesh):
    in_specs = (
        P("seq", "expert"),
        P("seq", "expert"),
        P("seq", "expert"),
        P(None, None, "seq"),
        P(None, "expert"),
        P(None, "expert"),
        P("expert"),
        P("expert"),
        P("expert"),
        P("expert", None),
        P(("seq", "expert"), None),
        P("expert", None, "seq"),
        P("expert", None, "seq"),
        P("expert", "seq", None),
        P(("seq", "expert"), None),
        P(("seq", "expert"), None),
        P("seq", None),
    )
    out_specs = (
        P(("seq", "expert"), None),
        P("seq", "expert"),
        P("seq", "expert"),
        P("seq", "expert"),
        P(None, None, "seq"),
        P(None, "expert"),
        P(None, "expert"),
        P(None, "expert"),
    )
    return jax.shard_map(local, mesh=mesh, in_specs=in_specs, out_specs=out_specs, check_vma=False)
```

profile of v0, /device:TPU:0, one launch (start us, length us, event | category | flops | bytes accessed | tf_op | source)
XLA Modules:
  0.0 318.6 jit_solution(18126991600475165741)
XLA Ops:
  7.2 0.0 all-reduce.3.cloned.1.call-start
  7.3 0.8 slice.144
  8.1 2.4 collective-permute-start
  10.5 0.8 copy.40
  11.3 1.5 exponential_negate_fusion.rate_ref
  12.8 3.8 %fusion.70 = f32[128,1024]{1,0:T(8,128)S(1)} fusion(bf16[128,2048]{1,0:T(8,128)(2,1)S(1)} %copy-done, bf16[1024,2048]{1,0:T(8,128)(2,1)} %param.26), kind=kOutput, calls=%fused_computation.128 | convolution fusion | flops 536870912 | bytes 5242880 | tf_op jit(solution)/shard_map/dot_general | solution.py:277
  16.7 1.3 multiply_reduce_fusion
  18.0 1.4 multiply_bitcast_fusion
  19.4 1.3 broadcast_in_dim.47.b_ref
  20.8 1.4 broadcast_in_dim.49.c_ref
  22.1 5.6 %totals.1 = bf16[3,16,1024]{2,1,0:T(8,128)(2,1)} custom-call(f32[16,8,1024]{2,1,0:T(8,128)} %get-tuple-element.42.step_ref, f32[16,8,1024]{2,1,0:T(8,128)} %get-tuple-element.41.drive_ref, f32[16,8,1024]{2,1,0:T(8,128)} %get-tuple-element.40.grad_ref, f32[16,8,16,128]{3,2,1,0:T(8,128)} %broadcast_in_dim.47.b_ref, f32[16,8,16,128]{3,2,1,0:T(8,128)} %broadcast_in_dim.49.c_ref, ...), custom_call_target="tpu_custom_call" | custom-call | tf_op jit(solution)/shard_map/totals/pallas_call | solution.py:294
  27.7 12.5 %all-gather = bf16[24,16,1024]{2,1,0:T(8,128)(2,1)S(1)} all-gather(bf16[3,16,1024]{2,1,0:T(8,128)(2,1)} %totals.1), channel_id=2, replica_groups=mesh['seq'=8,'expert'=4] {'seq'}, dimensions={0}, use_global_device_ids=true | all-gather | bytes 884736 | tf_op jit(solution)/shard_map/all_gather | solution.py:295
  40.2 0.2 convert
  40.4 0.7 fusion.47.start_ref
  41.1 6.0 %forward.1 = f32[16,8,1024]{2,1,0:T(8,128)} custom-call(f32[16,8,1024]{2,1,0:T(8,128)} %get-tuple-element.42.step_ref, f32[16,8,1024]{2,1,0:T(8,128)} %get-tuple-element.41.drive_ref, f32[16,8,16,128]{3,2,1,0:T(8,128)} %broadcast_in_dim.47.b_ref, f32[16,8,16,128]{3,2,1,0:T(8,128)} %broadcast_in_dim.49.c_ref, f32[16,1024]{1,0:T(8,128)} %exponential_negate_fusion.rate_ref, ...), custom_call_target="tpu_custom_call" | custom-call | tf_op jit(solution)/shard_map/forward/pallas_call | solution.py:296
  47.1 4.2 %convolution_convert_fusion = bf16[128,2048]{1,0:T(8,128)(2,1)} fusion(bf16[1024,2048]{1,0:T(8,128)(2,1)} %param.26, bf16[128,1024]{1,0:T(8,128)(2,1)} %param.18, f32[16,8,1024]{2,1,0:T(8,128)} %forward.1, f32[1024]{0:T(1024)S(1)} %copy-done.12, f32[128,1024]{1,0:T(8,128)S(1)} %get-tuple-element.37), kind=kOutput, calls=%fused_computation.7 | convolution fusion | flops 538836992 | bytes 6033408 | tf_op jit(solution)/shard_map/dot_general | solution.py:299
  51.3 0.0 all-gather.4.cloned.1.call-start
  51.4 23.4 %all_gather.15 = bf16[128,2048]{1,0:T(8,128)(2,1)} all-gather(bf16[32,2048]{1,0:T(8,128)(2,1)} %param.27), channel_id=1, replica_groups=mesh['seq'=8,'expert'=4] {'expert'}, dimensions={0}, use_global_device_ids=true | all-gather | bytes 655360 | tf_op jit(solution)/shard_map/all_gather | solution.py:191
  74.8 19.7 %all-reduce.3.cloned.1.call-done = bf16[128,2048]{1,0:T(8,128)(2,1)} async-done(((bf16[128,2048]{1,0:T(8,128)(2,1)}), bf16[128,2048]{1,0:T(8,128)(2,1)}) %all-reduce.3.cloned.1.call-update) | async-done | bytes 524304 | tf_op jit(solution)/shard_map/psum | solution.py:192
  94.5 2.1 add_convert_fusion
  96.7 0.0 reduce-scatter.3.cloned.1.call-start
  96.7 66.7 %all-gather.1 = f32[32,32,4]{1,2,0:T(4,128)S(1)} all-gather(f32[1,32,4]{1,2,0:T(4,128)S(1)} %bitcast.256), channel_id=1, replica_groups=mesh['seq'=8,'expert'=4] {'seq','expert'}, dimensions={0}, use_global_device_ids=true | all-gather | bytes 16896 | tf_op jit(solution)/shard_map/all_gather | solution.py:188
  163.5 0.1 reshape.73
  163.6 0.1 select_reduce_fusion
  163.7 7.5 %fusion.1 = f32[1024,896]{1,0:T(8,128)S(1)} fusion(bf16[1024,2048]{1,0:T(8,128)(2,1)} %all-gather.4.cloned.1.call-done, bf16[1,2048,896]{2,1,0:T(8,128)(2,1)} %param.29), kind=kOutput, calls=%fused_computation.2 | convolution fusion | flops 3758096384 | bytes 11534336 | tf_op jit(solution)/shard_map/dot_general | solution.py:196
  171.3 4.8 %multiply_convert_fusion.1 = bf16[1024,896]{1,0:T(8,128)(2,1)S(1)} fusion(f32[1024,896]{1,0:T(8,128)S(1)} %fusion.1, bf16[1024,2048]{1,0:T(8,128)(2,1)S(1)} %copy-done.15, bf16[1,2048,896]{2,1,0:T(8,128)(2,1)S(1)} %copy-done.16), kind=kOutput, calls=%fused_computation.6 | convolution fusion | flops 3763601408 | bytes 13369344 | tf_op jit(solution)/shard_map/dot_general | solution.py:195
  176.0 6.1 %multiply_convert_fusion = bf16[1024,2048]{1,0:T(8,128)(2,1)} fusion(bf16[1024,896]{1,0:T(8,128)(2,1)S(1)} %multiply_convert_fusion.1, f32[1024]{0:T(1024)S(1)} %select_reduce_fusion, bf16[1,896,2048]{2,1,0:T(8,128)(2,1)S(1)} %copy-done.17), kind=kOutput, calls=%fused_computation | convolution fusion | flops 3762290688 | bytes 9703424 | tf_op jit(solution)/shard_map/dot_general | solution.py:198
  182.1 0.2 all-reduce.5.cloned.1.call-start
  182.4 0.7 fusion.31.arriving_ref
  183.1 13.2 %backward.1 = (f32[16,8,1024]{2,1,0:T(8,128)}, f32[16,8,1024]{2,1,0:T(8,128)}, f32[16,8,16,128]{3,2,1,0:T(8,128)}, f32[16,8,16,128]{3,2,1,0:T(8,128)}, f32[16,1024]{1,0:T(8,128)}) custom-call(f32[16,8,1024]{2,1,0:T(8,128)} %get-tuple-element.42.step_ref, f32[16,8,1024]{2,1,0:T(8,128)} %get-tuple-element.41.drive_ref, ...), custom_call_target="tpu_custom_call" | custom-call | tf_op jit(solution)/shard_map/backward/pallas_call | solution.py:305
  196.3 2.0 fusion.67
  198.3 2.7 fusion.66
  201.0 1.3 concatenate.12
  202.3 0.0 reduce-scatter.5.cloned.1.call-start
  202.3 27.7 %reduce-scatter.3.cloned.1.call-done = bf16[128,2048]{1,0:T(8,128)(2,1)} async-done(((bf16[1024,2048]{1,0:T(8,128)(2,1)}), bf16[128,2048]{1,0:T(8,128)(2,1)}) %reduce-scatter.3.cloned.1.call-update) | async-done | bytes 524304 | tf_op jit(solution)/shard_map/reduce_scatter | solution.py:200
  230.1 1.6 reduce_sum.101
  231.7 0.1 copy.42
  231.7 1.6 reduce_sum.102
  233.3 0.1 copy.43
  233.4 1.3 collective-permute-start.1
  234.7 19.3 %psum.22 = f32[2,16,128]{2,1,0:T(8,128)} all-reduce(f32[2,16,128]{2,1,0:T(8,128)S(1)} %maximum_bitcast_fusion), channel_id=1, replica_groups=mesh['seq'=8,'expert'=4] {'expert'}, use_global_device_ids=true, to_apply=%region_7.8 | all-reduce | flops 4096 | bytes 32768 | tf_op jit(solution)/shard_map/psum | solution.py:327
  254.0 1.0 fusion.10
  255.0 30.6 %all-reduce.5.cloned.1.call-done = f32[23,1024]{1,0:T(8,128)} async-done(((f32[23,1024]{1,0:T(8,128)}), f32[23,1024]{1,0:T(8,128)}) %all-reduce.5.cloned.1.call-update) | async-done | bytes 94224 | tf_op jit(solution)/shard_map/psum | solution.py:322
  285.7 1.5 slice.219
  287.1 1.4 slice.220
  288.5 1.4 slice.221
  289.9 20.6 %reduce-scatter.5.cloned.1.call-done = bf16[32,2048]{1,0:T(8,128)(2,1)} async-done(((bf16[128,2048]{1,0:T(8,128)(2,1)}), bf16[32,2048]{1,0:T(8,128)(2,1)}) %reduce-scatter.5.cloned.1.call-update) | async-done | bytes 131088 | tf_op jit(solution)/shard_map/reduce_scatter | solution.py:201
  310.4 1.7 add_convert_fusion.1
  (53 shorter events, 0.3 us)
Async XLA Ops:
  7.2 5.6 %copy-start = (bf16[128,2048]{1,0:T(8,128)(2,1)S(1)}, bf16[128,2048]{1,0:T(8,128)(2,1)}, u32[]{:S(2)}) copy-start(bf16[128,2048]{1,0:T(8,128)(2,1)} %param.33) | copy-start | bytes 1572868
  7.2 9.4 %copy-start.6 = (bf16[128,1024]{1,0:T(8,128)(2,1)S(1)}, bf16[128,1024]{1,0:T(8,128)(2,1)}, u32[]{:S(2)}) copy-start(bf16[128,1024]{1,0:T(8,128)(2,1)} %param.17) | copy-start | bytes 786436
  7.2 9.4 %copy-start.10 = (f32[4,1024]{1,0:T(4,128)S(1)}, f32[4,1024]{1,0:T(4,128)}, u32[]{:S(2)}) copy-start(f32[4,1024]{1,0:T(4,128)} %param.22) | copy-start | bytes 49156
  7.2 9.5 %copy-start.7 = (bf16[128,1024]{1,0:T(8,128)(2,1)S(1)}, bf16[128,1024]{1,0:T(8,128)(2,1)}, u32[]{:S(2)}) copy-start(bf16[128,1024]{1,0:T(8,128)(2,1)} %param.18) | copy-start | bytes 786436
  7.2 9.5 %copy-start.11 = (f32[1024]{0:T(1024)S(1)}, f32[1024]{0:T(1024)}, u32[]{:S(2)}) copy-start(f32[1024]{0:T(1024)} %param.23) | copy-start | bytes 12292
  7.2 87.3 %all-reduce.3.cloned.1.call-start = ((), (), s32[]{:S(2)}) async-start(), calls=%async_computation.2 | async-start | bytes 1048576 | tf_op jit(solution)/shard_map/psum | solution.py:192
  8.1 8.6 %collective-permute-start = (bf16[3,1024]{1,0:T(4,128)(2,1)S(1)}, bf16[3,1024]{1,0:T(4,128)(2,1)S(1)}, u32[]{:S(2)}, u32[]{:S(2)}) collective-permute-start(bf16[3,1024]{1,0:T(4,128)(2,1)S(1)} %slice.144), channel_id=1, source_target_pairs={{0,4},{4,8},{8,12},{12,16},{16,20},{20,24},{24,28},{1,5},{5,9},{9,... | collective-permute-start | bytes 18440 | tf_op jit(solution)/shard_map/ppermute | solution.py:16
  12.8 5.2 %copy-start.3 = (f32[128,1024]{1,0:T(8,128)S(1)}, f32[128,1024]{1,0:T(8,128)}, u32[]{:S(2)}) copy-start(f32[128,1024]{1,0:T(8,128)} %param.19) | copy-start | bytes 1572868
  12.8 5.2 %copy-start.9 = (f32[1024]{0:T(1024)S(1)}, f32[1024]{0:T(1024)}, u32[]{:S(2)}) copy-start(f32[1024]{0:T(1024)} %param.25) | copy-start | bytes 12292
  16.6 11.1 %copy-start.1 = (f32[128,1024]{1,0:T(8,128)}, f32[128,1024]{1,0:T(8,128)S(1)}, u32[]{:S(2)}) copy-start(f32[128,1024]{1,0:T(8,128)S(1)} %convert_element_type.44) | copy-start | bytes 1572868
  40.2 6.9 %copy-start.12 = (f32[1024]{0:T(1024)S(1)}, f32[1024]{0:T(1024)}, u32[]{:S(2)}) copy-start(f32[1024]{0:T(1024)} %param.24) | copy-start | bytes 12292
  47.1 49.6 %copy-start.13 = (f32[32,2]{0,1:T(2,128)S(1)}, f32[32,2]{0,1:T(2,128)}, u32[]{:S(2)}) copy-start(f32[32,2]{0,1:T(2,128)} %param.32) | copy-start | bytes 772
  47.1 49.6 %copy-start.14 = (s32[32,2]{0,1:T(2,128)S(1)}, s32[32,2]{0,1:T(2,128)}, u32[]{:S(2)}) copy-start(s32[32,2]{0,1:T(2,128)} %param.31) | copy-start | bytes 772
  51.3 112.4 %all-gather.4.cloned.1.call-start = ((), (), s32[]{:S(2)}) async-start(), calls=%async_computation.3 | async-start | bytes 4718592 | tf_op jit(solution)/shard_map/all_gather | solution.py:194
  96.7 133.4 %reduce-scatter.3.cloned.1.call-start = ((), (), s32[]{:S(2)}) async-start(), calls=%async_computation.4 | async-start | bytes 4718592 | tf_op jit(solution)/shard_map/reduce_scatter | solution.py:200
  163.7 7.5 %copy-start.15 = (bf16[1024,2048]{1,0:T(8,128)(2,1)S(1)}, bf16[1024,2048]{1,0:T(8,128)(2,1)}, u32[]{:S(2)}) copy-start(bf16[1024,2048]{1,0:T(8,128)(2,1)} %all-gather.4.cloned.1.call-done) | copy-start | bytes 12582916
  163.7 7.5 %copy-start.16 = (bf16[1,2048,896]{2,1,0:T(8,128)(2,1)S(1)}, bf16[1,2048,896]{2,1,0:T(8,128)(2,1)}, u32[]{:S(2)}) copy-start(bf16[1,2048,896]{2,1,0:T(8,128)(2,1)} %param.28) | copy-start | bytes 11010052
  171.3 4.8 %copy-start.17 = (bf16[1,896,2048]{2,1,0:T(8,128)(2,1)S(1)}, bf16[1,896,2048]{2,1,0:T(8,128)(2,1)}, u32[]{:S(2)}) copy-start(bf16[1,896,2048]{2,1,0:T(8,128)(2,1)} %param.30) | copy-start | bytes 11010052
  182.1 103.5 %all-reduce.5.cloned.1.call-start = ((), (), s32[]{:S(2)}) async-start(), calls=%async_computation.6 | async-start | bytes 196608 | tf_op jit(solution)/shard_map/psum | solution.py:322
  183.0 13.3 %copy-start.4 = (f32[128,1024]{1,0:T(8,128)S(1)}, f32[128,1024]{1,0:T(8,128)}, u32[]{:S(2)}) copy-start(f32[128,1024]{1,0:T(8,128)} %param.19) | copy-start | bytes 1572868
  183.0 15.3 %copy-start.2 = (f32[128,1024]{1,0:T(8,128)S(1)}, f32[128,1024]{1,0:T(8,128)}, u32[]{:S(2)}) copy-start(f32[128,1024]{1,0:T(8,128)} %copy-done.1) | copy-start | bytes 1572868
  183.0 15.3 %copy-start.5 = (f32[16,8,1024]{2,1,0:T(8,128)S(1)}, f32[16,8,1024]{2,1,0:T(8,128)}, u32[]{:S(2)}) copy-start(f32[16,8,1024]{2,1,0:T(8,128)} %forward.1) | copy-start | bytes 1572868
  196.3 4.7 %copy-start.8 = (f32[16,1024]{1,0:T(8,128)S(1)}, f32[16,1024]{1,0:T(8,128)}, u32[]{:S(2)}) copy-start(f32[16,1024]{1,0:T(8,128)} %get-tuple-element.17) | copy-start | bytes 196612
  202.3 108.1 %reduce-scatter.5.cloned.1.call-start = ((), (), s32[]{:S(2)}) async-start(), calls=%async_computation.5 | async-start | bytes 655360 | tf_op jit(solution)/shard_map/reduce_scatter | solution.py:201
  233.4 20.6 %collective-permute-start.1 = (f32[3,1024]{1,0:T(4,128)S(1)}, f32[3,1024]{1,0:T(4,128)S(1)}, u32[]{:S(2)}, u32[]{:S(2)}) collective-permute-start(f32[3,1024]{1,0:T(4,128)S(1)} %slice.214), channel_id=1, source_target_pairs={{4,0},{8,4},{12,8},{16,12},{20,16},{24,20},{28,24},{5,1},{9,5},{13... | collective-permute-start | bytes 36872 | tf_op jit(solution)/shard_map/ppermute | solution.py:16
Sparse Core Ops, SparseCore 0:
  51.4 43.0 all-reduce.2
  96.8 36.4 all-gather.3
  182.2 47.7 reduce-scatter.2
  233.6 52.0 all-reduce.4
  287.8 22.5 reduce-scatter.4
where the time goes:
time: 319 us
  blocking collectives  122 us (38%)
  waiting for transfers between devices  98.7 us (31%)
  matrix products  26.2 us (8%)
  Pallas kernels  24.8 us (8%)
  other arithmetic  18.5 us (6%)
  between operations  14.1 us (4%)
  local copies, waits for them, and re-layouts  10.1 us (3%)
  starting transfers between devices  4.07 us (1%)
    all_gather x1, blocking collectives, dense_experts(): every_share = lax.all_gather(share, ('seq', 'expert'), axis=0, tiled=True)  66.7 us
    psum x1, waiting for transfers between devices, local(): lax.psum(jnp.concatenate([grad_alog_local, grad_taps, channel_grads], axi...  30.6 us
    reduce_scatter x1, waiting for transfers between devices, dense_experts(): group_sum = lax.psum_scatter(part, 'seq', scatter_dimension=0, tiled=True)  27.7 us
    all_gather x1, blocking collectives, dense_experts(): group_resid = lax.all_gather(resid, 'expert', axis=0, tiled=True)  23.4 us
    reduce_scatter x1, waiting for transfers between devices, dense_experts(): moe = lax.psum_scatter(group_sum, 'expert', scatter_dimension=0, tiled=True)  20.6 us
    psum x1, waiting for transfers between devices, dense_experts(): mixed = lax.psum(partial_value, 'expert')  19.7 us
    psum x1, blocking collectives, local(): lax.psum(grad_bc.reshape(2, length, states).transpose(0, 2, 1), 'expert')  19.3 us
    pallas_call x1, Pallas kernels, local(): backward(step_g, drive_g, conv_g, grad_g, b_wide, c_wide, rate, start, ar...  13.2 us
  transfers between devices with their start and end apart: 7, of which 4 were waited for; matrix products, arithmetic and copies ran while one was open for 7% of the time, Pallas kernels for 4%

commit v1 on v0

--- a/solution.py
+++ b/solution.py
@@ -6,6 +6,7 @@
 from jax.sharding import PartitionSpec as P
 
 KW = 4
+WHOLE_GATHER = False
 SUB = 8
 LANES = 128
 
@@ -179,28 +180,25 @@
     return start, arriving
 
 
-def dense_experts(partial_value, resid, w_gate, w_up, w_down, route_ids, route_weight):
-    rows = resid.shape[0]
+def group_shares(route_ids, route_weight, rows):
     experts = lax.axis_size("expert")
-    mine = lax.axis_index("expert")
     chosen = route_ids[:, :, None] == jnp.arange(experts, dtype=jnp.int32)[None, None, :]
     share = jnp.sum(jnp.where(chosen, route_weight[:, :, None], 0.0), axis=1)
-    every_share = lax.all_gather(share, ("seq", "expert"), axis=0, tiled=True)
-    is_mine = jnp.arange(experts, dtype=jnp.int32)[None, :] == mine
-    scale = jnp.sum(jnp.where(is_mine, every_share, 0.0), axis=1, keepdims=True)
-    group_resid = lax.all_gather(resid, "expert", axis=0, tiled=True)
-    mixed = lax.psum(partial_value, "expert")
-    hidden_in = (group_resid.astype(jnp.float32) + mixed.astype(jnp.float32)).astype(jnp.bfloat16)
-    piece = lax.all_gather(hidden_in, "seq", axis=0, tiled=True)
+    own = (jnp.arange(experts) == lax.axis_index("expert")).astype(jnp.float32)
+    return (own[None, :, None] * share.T[:, None, :]).reshape(experts, experts * rows)
+
+
+def dense_experts(hidden_in, piece, shares, w_gate, w_up, w_down, rows):
+    mine = lax.axis_index("expert")
     gate = jnp.dot(piece, w_gate[0], preferred_element_type=jnp.float32)
     upper = jnp.dot(piece, w_up[0], preferred_element_type=jnp.float32)
     hidden = (jax.nn.silu(gate) * upper).astype(jnp.bfloat16)
-    part = jnp.dot(hidden, w_down[0], preferred_element_type=jnp.float32)
-    part = (part * scale).astype(jnp.bfloat16)
+    part = jnp.dot(hidden, w_down[0], preferred_element_type=jnp.float32).astype(jnp.bfloat16)
     group_sum = lax.psum_scatter(part, "seq", scatter_dimension=0, tiled=True)
-    moe = lax.psum_scatter(group_sum, "expert", scatter_dimension=0, tiled=True)
-    own = lax.dynamic_slice_in_dim(hidden_in, mine * rows, rows, 0)
-    return (own.astype(jnp.float32) + moe.astype(jnp.float32)).astype(jnp.bfloat16)
+    scale = lax.dynamic_index_in_dim(shares, mine, 0, keepdims=False)[:, None]
+    weighted = (group_sum.astype(jnp.float32) * scale).astype(jnp.bfloat16)
+    moe = lax.psum_scatter(weighted, "expert", scatter_dimension=0, tiled=True)
+    return (hidden_in.astype(jnp.float32) + moe.astype(jnp.float32)).astype(jnp.bfloat16)
 
 
 def routed_experts(partial_value, resid, w_gate, w_up, w_down, route_ids, route_weight):
@@ -296,11 +294,19 @@
     y_val = flat(forward(step_g, drive_g, b_wide, c_wide, rate, start))
     y_val = y_val + skip_gain[None, :] * conv_out
     gated = (y_val * z_val * z_sig).astype(jnp.bfloat16)
-    partial_value = jnp.dot(gated, out_weight, preferred_element_type=jnp.float32).astype(
-        jnp.bfloat16
-    )
-    experts = dense_experts if lax.axis_size("expert") <= 4 else routed_experts
-    layer_out = experts(partial_value, resid, w_gate, w_up, w_down, route_ids, route_weight)
+    partial_value = jnp.dot(gated, out_weight, preferred_element_type=jnp.float32)
+    rows = resid.shape[0]
+    mine = lax.axis_index("expert")
+    experts = lax.axis_size("expert")
+    dense = experts <= 4
+    if dense:
+        own_rows = (jnp.arange(experts) == mine).astype(jnp.float32)[:, None, None]
+        placed = (own_rows * resid.astype(jnp.float32)[None]).reshape(partial_value.shape)
+        partial_value = (partial_value + placed).astype(jnp.bfloat16)
+        if WHOLE_GATHER:
+            summed = lax.psum_scatter(partial_value, "expert", scatter_dimension=0, tiled=True)
+        else:
+            summed = lax.psum(partial_value, "expert")
     grad_z = back_mix * y_val * z_sig * (1.0 + z_val * (1.0 - z_sig))
     grad_step, conv_part_grad, grad_b, grad_c, grad_alog_local = backward(
         step_g, drive_g, conv_g, grad_g, b_wide, c_wide, rate, start, arriving
@@ -319,12 +325,43 @@
         [jnp.sum(grad_pre * padded[tap : tap + length], axis=0) for tap in range(KW)]
     )
     channel_grads = jnp.stack([jnp.sum(grad_pre, axis=0), grad_skip, jnp.sum(grad_dt, axis=0)])
-    sums = lax.psum(jnp.concatenate([grad_alog_local, grad_taps, channel_grads], axis=0), "seq")
+    own_sums = jnp.concatenate([grad_alog_local, grad_taps, channel_grads], axis=0)
+    own_bc = jnp.stack([jnp.sum(grad_b, axis=-1), jnp.sum(grad_c, axis=-1)])
+    own_bc = own_bc.reshape(2, length, states).transpose(0, 2, 1).reshape(2 * states, length)
+    if dense:
+        if WHOLE_GATHER:
+            summed, own_sums = lax.optimization_barrier((summed, own_sums))
+            hidden_in = summed
+            piece = lax.all_gather(hidden_in, ("seq", "expert"), axis=0, tiled=True)
+            sums = jnp.sum(lax.all_gather(own_sums, "seq"), axis=0)
+        else:
+            sums = lax.all_gather(own_sums, "seq")
+            summed, sums = lax.optimization_barrier((summed, sums))
+            sums = jnp.sum(sums, axis=0)
+            hidden_in = lax.dynamic_slice_in_dim(summed, mine * rows, rows, 0)
+            piece = lax.all_gather(summed, "seq", axis=0, tiled=True)
+        shares = group_shares(route_ids, route_weight, rows)
+        joined = lax.psum(jnp.concatenate([own_bc, shares], axis=0), "expert")
+        piece, joined, sums = lax.optimization_barrier((piece, joined, sums))
+        grad_bc = joined[: 2 * states].reshape(2, states, length)
+        layer_out = dense_experts(
+            hidden_in, piece, joined[2 * states :], w_gate, w_up, w_down, rows
+        )
+    else:
+        layer_out = routed_experts(
+            partial_value.astype(jnp.bfloat16),
+            resid,
+            w_gate,
+            w_up,
+            w_down,
+            route_ids,
+            route_weight,
+        )
+        sums = lax.psum(own_sums, "seq")
+        grad_bc = lax.psum(own_bc, "expert").reshape(2, states, length)
     grad_alog = sums[:states]
     grad_conv = sums[states : states + KW]
     grad_chan = sums[states + KW :]
-    grad_bc = jnp.stack([jnp.sum(grad_b, axis=-1), jnp.sum(grad_c, axis=-1)])
-    grad_bc = lax.psum(grad_bc.reshape(2, length, states).transpose(0, 2, 1), "expert")
     return (layer_out, grad_x, grad_z, grad_dt, grad_bc, grad_alog, grad_conv, grad_chan)
 
 

time: 319 us -> 236 us (0.74)
  blocking collectives: 122 us -> 40.5 us
    all_gather x2 -> x1, blocking collectives: 90.2 us -> 10.1 us  [local(): sums = lax.all_gather(own_sums, 'seq')]
    psum x2 -> x1, waiting for transfers between devices: 50.3 us -> 10.4 us  [local(): summed = lax.psum(partial_value, 'expert')]
    reduce_scatter x1, waiting for transfers between devices: 27.7 us -> 51.2 us  [dense_experts(): group_sum = lax.psum_scatter(part, 'seq', scatter_dimension=0, tiled=True)]
    all_gather x1, waiting for transfers between devices: 0.02 us -> 16.9 us  [local(): piece = lax.all_gather(summed, 'seq', axis=0, tiled=True)]
    reduce_scatter x1, waiting for transfers between devices: 20.6 us -> 15.4 us  [dense_experts(): moe = lax.psum_scatter(weighted, 'expert', scatter_dimension=0, tiled=True)]
  transfers between devices with their start and end apart: 7 -> 6, of which waited for: 4 -> 5; matrix products, arithmetic and copies ran while one was open for 7% -> 9% of each run, Pallas kernels for 4% -> 5%
where the time goes in v1:
time: 236 us; the launch traced here: 235 us
  waiting for transfers between devices  95.7 us (41%)
  blocking collectives  40.5 us (17%)
  matrix products  26.5 us (11%)
  Pallas kernels  24.4 us (10%)
  other arithmetic  21.5 us (9%)
  between operations  14.2 us (6%)
  local copies, waits for them, and re-layouts  8.77 us (4%)
  starting transfers between devices  3.84 us (2%)
    reduce_scatter x1, waiting for transfers between devices, dense_experts(): group_sum = lax.psum_scatter(part, 'seq', scatter_dimension=0, tiled=True)  51.2 us
    psum x1, blocking collectives, local(): joined = lax.psum(jnp.concatenate([own_bc, shares], axis=0), 'expert')  17.9 us
    all_gather x1, waiting for transfers between devices, local(): piece = lax.all_gather(summed, 'seq', axis=0, tiled=True)  16.9 us
    reduce_scatter x1, waiting for transfers between devices, dense_experts(): moe = lax.psum_scatter(weighted, 'expert', scatter_dimension=0, tiled=True)  15.4 us
    pallas_call x1, Pallas kernels, local(): backward(step_g, drive_g, conv_g, grad_g, b_wide, c_wide, rate, start, ar...  12.8 us
    all_gather x1, blocking collectives, local(): start, arriving = entering(lax.all_gather(own_totals, 'seq'))  12.5 us
    psum x1, waiting for transfers between devices, local(): summed = lax.psum(partial_value, 'expert')  10.4 us
    all_gather x1, blocking collectives, local(): sums = lax.all_gather(own_sums, 'seq')  10.1 us
  transfers between devices with their start and end apart: 6, of which 5 were waited for; matrix products, arithmetic and copies ran while one was open for 9% of the time, Pallas kernels for 5%

profile of v1, /device:TPU:0, one launch (start us, length us, event | category | flops | bytes accessed | tf_op | source)
XLA Modules:
  0.0 235.4 jit_solution(11413146290997499368)
XLA Ops:
  7.2 0.8 slice.150
  8.0 2.4 %collective-permute-start = (bf16[3,1024]{1,0:T(4,128)(2,1)S(1)}, bf16[3,1024]{1,0:T(4,128)(2,1)S(1)}, u32[]{:S(2)}, u32[]{:S(2)}) collective-permute-start(bf16[3,1024]{1,0:T(4,128)(2,1)S(1)} %slice.150), channel_id=1, source_target_pairs={{0,4},{4,8},{8,12},{12,16},{16,20},{20,24},{24,28},{1,5},{5,9},{9,... | collective-permute-start | bytes 18440 | tf_op jit(solution)/shard_map/ppermute | solution.py:17
  10.4 1.5 fusion.70
  11.9 1.5 exponential_negate_fusion.rate_ref
  13.4 0.8 copy.41
  14.3 3.7 %fusion.71 = f32[128,1024]{1,0:T(8,128)S(1)} fusion(bf16[128,2048]{1,0:T(8,128)(2,1)S(1)} %copy-done, bf16[1024,2048]{1,0:T(8,128)(2,1)} %param.26), kind=kOutput, calls=%fused_computation.132 | convolution fusion | flops 536870912 | bytes 5242880 | tf_op jit(solution)/shard_map/dot_general | solution.py:275
  18.1 0.1 mul.267
  18.2 0.1 mul.268
  18.3 1.1 bitcast_multiply_fusion
  19.5 2.6 %multiply_reduce_fusion = (f32[1024]{0:T(1024)}, f32[128,1024]{1,0:T(8,128)S(1)}, f32[16,8,1024]{2,1,0:T(8,128)}) fusion(f32[128,1024]{1,0:T(8,128)S(1)} %fusion.71, bf16[128,1024]{1,0:T(8,128)(2,1)S(1)} %copy-done.7, f32[128,1024]{1,0:T(8,128)S(1)} %convert_element_type.55, f32[1024]{0:T(1024)} %bitcast.252, f32[3,1024]{1,0:T(4,128)S(1)} %convert_element_type.54, ...), kind=kLoop, calls=%fused_computation.48 | loop fusion | flops 3013632 | bytes 2396160 | tf_op jit(solution)/shard_map/reduce_sum | solution.py:316
  22.1 2.1 multiply_bitcast_fusion
  24.2 1.4 broadcast_in_dim.23.c_ref
  25.6 1.3 broadcast_in_dim.17.b_ref
  26.9 5.6 %totals.1 = bf16[3,16,1024]{2,1,0:T(8,128)(2,1)} custom-call(f32[16,8,1024]{2,1,0:T(8,128)} %get-tuple-element.44.step_ref, f32[16,8,1024]{2,1,0:T(8,128)} %get-tuple-element.43.drive_ref, f32[16,8,1024]{2,1,0:T(8,128)} %get-tuple-element.42.grad_ref, f32[16,8,16,128]{3,2,1,0:T(8,128)} %broadcast_in_dim.17.b_ref, f32[16,8,16,128]{3,2,1,0:T(8,128)} %broadcast_in_dim.23.c_ref, ...), custom_call_target="tpu_custom_call" | custom-call | tf_op jit(solution)/shard_map/totals/pallas_call | solution.py:292
  32.5 12.5 %all-gather = bf16[24,16,1024]{2,1,0:T(8,128)(2,1)S(1)} all-gather(bf16[3,16,1024]{2,1,0:T(8,128)(2,1)} %totals.1), channel_id=2, replica_groups=mesh['seq'=8,'expert'=4] {'seq'}, dimensions={0}, use_global_device_ids=true | all-gather | bytes 884736 | tf_op jit(solution)/shard_map/all_gather | solution.py:293
  45.0 0.2 convert
  45.2 0.7 fusion.48.start_ref
  45.9 6.0 %forward.1 = f32[16,8,1024]{2,1,0:T(8,128)} custom-call(f32[16,8,1024]{2,1,0:T(8,128)} %get-tuple-element.44.step_ref, f32[16,8,1024]{2,1,0:T(8,128)} %get-tuple-element.43.drive_ref, f32[16,8,16,128]{3,2,1,0:T(8,128)} %broadcast_in_dim.17.b_ref, f32[16,8,16,128]{3,2,1,0:T(8,128)} %broadcast_in_dim.23.c_ref, f32[16,1024]{1,0:T(8,128)} %exponential_negate_fusion.rate_ref, ...), custom_call_target="tpu_custom_call" | custom-call | tf_op jit(solution)/shard_map/forward/pallas_call | solution.py:294
  51.9 4.4 %fusion.7 = bf16[128,2048]{1,0:T(8,128)(2,1)} fusion(f32[128,2048]{1,0:T(8,128)} %bitcast_multiply_fusion, bf16[1024,2048]{1,0:T(8,128)(2,1)} %param.26, bf16[128,1024]{1,0:T(8,128)(2,1)} %param.18, f32[16,8,1024]{2,1,0:T(8,128)} %forward.1, f32[1024]{0:T(1024)S(1)} %copy-done.18, f32[128,1024]{1,0:T(8,128)S(1)} %get-tuple-element.39), kind=kOutput, calls=%fused_computation.8 | convolution fusion | flops 539099136 | bytes 7081984 | tf_op jit(solution)/shard_map/dot_general | solution.py:297
  56.4 0.0 all-gather.5.cloned.1.call-start
  56.4 0.7 fusion.32.arriving_ref
  57.1 12.8 %backward.1 = (f32[16,8,1024]{2,1,0:T(8,128)}, f32[16,8,1024]{2,1,0:T(8,128)}, f32[16,8,16,128]{3,2,1,0:T(8,128)}, f32[16,8,16,128]{3,2,1,0:T(8,128)}, f32[16,1024]{1,0:T(8,128)}) custom-call(f32[16,8,1024]{2,1,0:T(8,128)} %get-tuple-element.44.step_ref, f32[16,8,1024]{2,1,0:T(8,128)} %get-tuple-element.43.drive_ref, ...), custom_call_target="tpu_custom_call" | custom-call | tf_op jit(solution)/shard_map/backward/pallas_call | solution.py:311
  70.0 2.0 fusion.68
  72.0 2.7 %fusion.67 = (f32[1024]{0:T(1024)S(1)}, f32[1024]{0:T(1024)S(1)}, f32[1024]{0:T(1024)S(1)}, f32[1024]{0:T(1024)S(1)}, f32[1024]{0:T(1024)S(1)}, /*index=5*/f32[128,1024]{1,0:T(8,128)S(1)}, f32[128,1024]{1,0:T(8,128)}) fusion(bf16[128,1024]{1,0:T(8,128)(2,1)S(1)} %copy-done.6, f32[128,1024]{1,0:T(8,128)S(1)} %copy-done.2, ...), kind=kLoop, calls=%fused_computation.129 | loop fusion | flops 4975616 | bytes 4231168 | tf_op jit(solution)/shard_map/reduce_sum | solution.py:327
  74.7 0.1 concatenate.14
  74.7 10.1 %all-gather.2 = f32[8,23,1024]{2,1,0:T(8,128)S(1)} all-gather(f32[1,23,1024]{2,1,0:T(8,128)S(1)} %bitcast.244), channel_id=3, replica_groups=mesh['seq'=8,'expert'=4] {'seq'}, dimensions={0}, use_global_device_ids=true | all-gather | bytes 847872 | tf_op jit(solution)/shard_map/all_gather | solution.py:338
  84.9 10.4 %all-reduce.2.cloned.1.call-done = bf16[128,2048]{1,0:T(8,128)(2,1)} async-done(((bf16[128,2048]{1,0:T(8,128)(2,1)}), bf16[128,2048]{1,0:T(8,128)(2,1)}) %all-reduce.2.cloned.1.call-update) | async-done | bytes 524304 | tf_op jit(solution)/shard_map/psum | solution.py:309
  95.4 0.1 mul.294
  95.5 1.6 reduce_sum.106
  97.1 0.1 copy.42
  97.1 1.6 reduce_sum.107
  98.7 0.1 copy.43
  98.8 17.9 %psum.15 = f32[36,128]{1,0:T(8,128)S(1)} all-reduce(f32[36,128]{1,0:T(8,128)S(1)} %pad_maximum_fusion.2), channel_id=1, replica_groups=mesh['seq'=8,'expert'=4] {'expert'}, use_global_device_ids=true, to_apply=%region_11.12 | all-reduce | flops 4608 | bytes 36864 | tf_op jit(solution)/shard_map/psum | solution.py:344
  116.7 16.9 %all-gather.5.cloned.1.call-done = bf16[1024,2048]{1,0:T(8,128)(2,1)} async-done(((bf16[128,2048]{1,0:T(8,128)(2,1)}), bf16[1024,2048]{1,0:T(8,128)(2,1)}) %all-gather.5.cloned.1.call-update) | async-done | bytes 4194320 | tf_op jit(solution)/shard_map/all_gather | solution.py:342
  133.6 7.5 %fusion.1 = f32[1024,896]{1,0:T(8,128)S(1)} fusion(bf16[1024,2048]{1,0:T(8,128)(2,1)} %all-gather.5.cloned.1.call-done, bf16[1,2048,896]{2,1,0:T(8,128)(2,1)} %param.29), kind=kOutput, calls=%fused_computation.2 | convolution fusion | flops 3758096384 | bytes 11534336 | tf_op jit(solution)/shard_map/dot_general | solution.py:194
  141.1 4.7 %multiply_convert_fusion = bf16[1024,896]{1,0:T(8,128)(2,1)S(1)} fusion(f32[1024,896]{1,0:T(8,128)S(1)} %fusion.1, bf16[1024,2048]{1,0:T(8,128)(2,1)S(1)} %copy-done.21, bf16[1,2048,896]{2,1,0:T(8,128)(2,1)S(1)} %copy-done.22), kind=kOutput, calls=%fused_computation.6 | convolution fusion | flops 3763601408 | bytes 13369344 | tf_op jit(solution)/shard_map/dot_general | solution.py:193
  145.9 6.0 %convolution_convert_fusion = bf16[1024,2048]{1,0:T(8,128)(2,1)} fusion(bf16[1024,896]{1,0:T(8,128)(2,1)S(1)} %multiply_convert_fusion, bf16[1,896,2048]{2,1,0:T(8,128)(2,1)S(1)} %copy-done.23), kind=kOutput, calls=%fused_computation | convolution fusion | flops 3760193536 | bytes 9699328 | tf_op jit(solution)/shard_map/dot_general | solution.py:196
  152.0 51.2 %reduce-scatter.3.cloned.1.call-done = bf16[128,2048]{1,0:T(8,128)(2,1)} async-done(((bf16[1024,2048]{1,0:T(8,128)(2,1)}), bf16[128,2048]{1,0:T(8,128)(2,1)}) %reduce-scatter.3.cloned.1.call-update) | async-done | bytes 524304 | tf_op jit(solution)/shard_map/reduce_scatter | solution.py:197
  203.3 2.0 multiply_convert_fusion.1
  205.3 1.3 collective-permute-start.1
  206.6 1.8 collective-permute-done.1
  208.4 1.0 fusion.11
  209.4 0.6 slice.188
  210.0 0.6 slice.191
  210.6 0.6 slice.190
  211.2 0.6 slice.189
  211.9 15.4 %reduce-scatter.5.cloned.1.call-done = bf16[32,2048]{1,0:T(8,128)(2,1)} async-done(((bf16[128,2048]{1,0:T(8,128)(2,1)}), bf16[32,2048]{1,0:T(8,128)(2,1)}) %reduce-scatter.5.cloned.1.call-update) | async-done | bytes 131088 | tf_op jit(solution)/shard_map/reduce_scatter | solution.py:200
  227.2 1.7 add_convert_fusion
  (70 shorter events, 0.5 us)
Async XLA Ops:
  7.2 7.1 %copy-start = (bf16[128,2048]{1,0:T(8,128)(2,1)S(1)}, bf16[128,2048]{1,0:T(8,128)(2,1)}, u32[]{:S(2)}) copy-start(bf16[128,2048]{1,0:T(8,128)(2,1)} %param.33) | copy-start | bytes 1572868
  7.2 10.9 %copy-start.6 = (bf16[128,1024]{1,0:T(8,128)(2,1)S(1)}, bf16[128,1024]{1,0:T(8,128)(2,1)}, u32[]{:S(2)}) copy-start(bf16[128,1024]{1,0:T(8,128)(2,1)} %param.17) | copy-start | bytes 786436
  7.2 11.1 %copy-start.8 = (bf16[32,2048]{1,0:T(8,128)(2,1)S(1)}, bf16[32,2048]{1,0:T(8,128)(2,1)}, u32[]{:S(2)}) copy-start(bf16[32,2048]{1,0:T(8,128)(2,1)} %param.27) | copy-start | bytes 393220
  7.2 88.1 %all-reduce.2.cloned.1.call-start = ((), (), s32[]{:S(2)}) async-start(), calls=%async_computation.2 | async-start | bytes 1048576 | tf_op jit(solution)/shard_map/psum | solution.py:309
  8.0 11.4 %collective-permute-start = (bf16[3,1024]{1,0:T(4,128)(2,1)S(1)}, bf16[3,1024]{1,0:T(4,128)(2,1)S(1)}, u32[]{:S(2)}, u32[]{:S(2)}) collective-permute-start(bf16[3,1024]{1,0:T(4,128)(2,1)S(1)} %slice.150), channel_id=1, source_target_pairs={{0,4},{4,8},{8,12},{12,16},{16,20},{20,24},{24,28},{1,5},{5,9},{9,... | collective-permute-start | bytes 18440 | tf_op jit(solution)/shard_map/ppermute | solution.py:17
  14.2 5.2 %copy-start.7 = (bf16[128,1024]{1,0:T(8,128)(2,1)S(1)}, bf16[128,1024]{1,0:T(8,128)(2,1)}, u32[]{:S(2)}) copy-start(bf16[128,1024]{1,0:T(8,128)(2,1)} %param.18) | copy-start | bytes 786436
  18.0 4.1 %copy-start.3 = (f32[128,1024]{1,0:T(8,128)S(1)}, f32[128,1024]{1,0:T(8,128)}, u32[]{:S(2)}) copy-start(f32[128,1024]{1,0:T(8,128)} %param.19) | copy-start | bytes 1572868
  18.1 7.5 %copy-start.1 = (f32[128,1024]{1,0:T(8,128)}, f32[128,1024]{1,0:T(8,128)S(1)}, u32[]{:S(2)}) copy-start(f32[128,1024]{1,0:T(8,128)S(1)} %convert_element_type.55) | copy-start | bytes 1572868
  18.3 1.2 copy-start.16
  45.0 6.9 %copy-start.18 = (f32[1024]{0:T(1024)S(1)}, f32[1024]{0:T(1024)}, u32[]{:S(2)}) copy-start(f32[1024]{0:T(1024)} %param.24) | copy-start | bytes 12292
  56.3 13.6 %copy-start.14 = (f32[1024]{0:T(1024)S(1)}, f32[1024]{0:T(1024)}, u32[]{:S(2)}) copy-start(f32[1024]{0:T(1024)} %param.25) | copy-start | bytes 12292
  56.4 77.2 %all-gather.5.cloned.1.call-start = ((), (), s32[]{:S(2)}) async-start(), calls=%async_computation.3 | async-start | bytes 4718592 | tf_op jit(solution)/shard_map/all_gather | solution.py:342
  57.1 12.9 %copy-start.4 = (f32[128,1024]{1,0:T(8,128)S(1)}, f32[128,1024]{1,0:T(8,128)}, u32[]{:S(2)}) copy-start(f32[128,1024]{1,0:T(8,128)} %param.19) | copy-start | bytes 1572868
  57.1 14.9 %copy-start.2 = (f32[128,1024]{1,0:T(8,128)S(1)}, f32[128,1024]{1,0:T(8,128)}, u32[]{:S(2)}) copy-start(f32[128,1024]{1,0:T(8,128)} %copy-done.1) | copy-start | bytes 1572868
  57.1 14.9 %copy-start.5 = (f32[16,8,1024]{2,1,0:T(8,128)S(1)}, f32[16,8,1024]{2,1,0:T(8,128)}, u32[]{:S(2)}) copy-start(f32[16,8,1024]{2,1,0:T(8,128)} %forward.1) | copy-start | bytes 1572868
  70.0 4.7 %copy-start.9 = (f32[16,1024]{1,0:T(8,128)S(1)}, f32[16,1024]{1,0:T(8,128)}, u32[]{:S(2)}) copy-start(f32[16,1024]{1,0:T(8,128)} %get-tuple-element.18) | copy-start | bytes 196612
  70.0 4.7 %copy-start.15 = (f32[1024]{0:T(1024)S(1)}, f32[1024]{0:T(1024)}, u32[]{:S(2)}) copy-start(f32[1024]{0:T(1024)} %get-tuple-element.38) | copy-start | bytes 12292
  70.0 25.4 %copy-start.19 = (f32[32,2]{0,1:T(2,128)S(1)}, f32[32,2]{0,1:T(2,128)}, u32[]{:S(2)}) copy-start(f32[32,2]{0,1:T(2,128)} %param.32) | copy-start | bytes 772
  70.0 25.4 %copy-start.20 = (s32[32,2]{0,1:T(2,128)S(1)}, s32[32,2]{0,1:T(2,128)}, u32[]{:S(2)}) copy-start(s32[32,2]{0,1:T(2,128)} %param.31) | copy-start | bytes 772
  70.0 25.5 %copy-start.17 = (f32[128]{0:T(128)S(1)}, f32[128]{0:T(128)}, u32[]{:S(2)}) copy-start(f32[128]{0:T(128)} %copy-done.16) | copy-start | bytes 1540
  95.3 108.0 %reduce-scatter.3.cloned.1.call-start = ((), (), s32[]{:S(2)}) async-start(), calls=%async_computation.4 | async-start | bytes 4718592 | tf_op jit(solution)/shard_map/reduce_scatter | solution.py:197
  133.6 7.5 %copy-start.21 = (bf16[1024,2048]{1,0:T(8,128)(2,1)S(1)}, bf16[1024,2048]{1,0:T(8,128)(2,1)}, u32[]{:S(2)}) copy-start(bf16[1024,2048]{1,0:T(8,128)(2,1)} %all-gather.5.cloned.1.call-done) | copy-start | bytes 12582916
  133.6 7.5 %copy-start.22 = (bf16[1,2048,896]{2,1,0:T(8,128)(2,1)S(1)}, bf16[1,2048,896]{2,1,0:T(8,128)(2,1)}, u32[]{:S(2)}) copy-start(bf16[1,2048,896]{2,1,0:T(8,128)(2,1)} %param.28) | copy-start | bytes 11010052
  141.1 4.8 %copy-start.23 = (bf16[1,896,2048]{2,1,0:T(8,128)(2,1)S(1)}, bf16[1,896,2048]{2,1,0:T(8,128)(2,1)}, u32[]{:S(2)}) copy-start(bf16[1,896,2048]{2,1,0:T(8,128)(2,1)} %param.30) | copy-start | bytes 11010052
  151.9 56.4 %copy-start.10 = (f32[1,1024]{1,0:T(1,128)S(1)}, f32[1,1024]{1,0:T(1,128)}, u32[]{:S(2)}) copy-start(f32[1,1024]{1,0:T(1,128)} %get-tuple-element.48) | copy-start | bytes 12292
  151.9 56.4 %copy-start.11 = (f32[1,1024]{1,0:T(1,128)S(1)}, f32[1,1024]{1,0:T(1,128)}, u32[]{:S(2)}) copy-start(f32[1,1024]{1,0:T(1,128)} %get-tuple-element.49) | copy-start | bytes 12292
  151.9 56.4 %copy-start.12 = (f32[1,1024]{1,0:T(1,128)S(1)}, f32[1,1024]{1,0:T(1,128)}, u32[]{:S(2)}) copy-start(f32[1,1024]{1,0:T(1,128)} %get-tuple-element.50) | copy-start | bytes 12292
  151.9 56.4 %copy-start.13 = (f32[1,1024]{1,0:T(1,128)S(1)}, f32[1,1024]{1,0:T(1,128)}, u32[]{:S(2)}) copy-start(f32[1,1024]{1,0:T(1,128)} %get-tuple-element.51) | copy-start | bytes 12292
  152.0 75.3 %reduce-scatter.5.cloned.1.call-start = ((), (), s32[]{:S(2)}) async-start(), calls=%async_computation.5 | async-start | bytes 655360 | tf_op jit(solution)/shard_map/reduce_scatter | solution.py:200
  205.3 3.1 %collective-permute-start.1 = (f32[3,1024]{1,0:T(4,128)S(1)}, f32[3,1024]{1,0:T(4,128)S(1)}, u32[]{:S(2)}, u32[]{:S(2)}) collective-permute-start(f32[3,1024]{1,0:T(4,128)S(1)} %slice.222), channel_id=1, source_target_pairs={{4,0},{8,4},{12,8},{16,12},{20,16},{24,20},{28,24},{5,1},{9,5},{13... | collective-permute-start | bytes 36872 | tf_op jit(solution)/shard_map/ppermute | solution.py:17
Sparse Core Ops, SparseCore 0:
  56.5 38.7 all-reduce.1
  97.2 36.3 all-gather.4
  152.1 51.1 reduce-scatter.2
  205.4 21.8 reduce-scatter.4
